TPU v7x, 256 devices: a whole 4x4x8 slice. The times are simulated.
256 devices in a mesh: ctx: 64 (over x_lo, y, z), kvh: 4 (over x_hi, core).
Axes of the slice: x: 4 (x_hi: 2, x_lo: 2; x = x_hi * 2 + x_lo), y: 4, z: 8, core: 2. Of those that a mesh axis runs over, the one named last changes fastest.
Arguments:
- queries: bfloat16 [16384, 2048], P(('ctx', 'kvh')), may hold values from -42 to 42
- keys: bfloat16 [16384, 512], P(('ctx', 'kvh')), may hold values from -6 to 6
- values: bfloat16 [16384, 512], P(('ctx', 'kvh')), may hold values from -6 to 6
- doc_lengths: int32 [16], replicated, may hold values from 1 to 8192, 16384 in all
Outputs:
- attended: bfloat16 [16384, 2048], P(('ctx', 'kvh'))
Inputs may be any that keep to these rules, and one draw needn't show every extreme that they name: `doc_lengths`: positive lengths that sum to 16384.
All inputs are finite; a program needn't handle non-finite values.
Results may differ from a plain program's by a relative error of at most 0.005.
Values may be sent and summed in bfloat16 or wider, within the bound.
No kernel may reach another device: no remote copies, remote signals or barrier semaphores. Data moves between devices by JAX's collectives and lax.ppermute only.
A program may use at most 64 MiB of HBM per device.

v0:
```python
import jax
import jax.numpy as jnp
from jax import lax
from jax.sharding import Mesh
from jax.sharding import PartitionSpec as P

HEAD_SIZE = 128
SINK = 128
CTX = ("ctx_0", "ctx_1", "ctx_2")
CTX_KVH = ("ctx_0", "ctx_1", "ctx_2", "kvh")


def side_by_side(arrays, axis, dim, along):
    both = jnp.concatenate(arrays, axis=along)
    out, at, outs = (lax.all_gather(both, axis, axis=dim, tiled=True), 0, [])
    for a in arrays:
        outs.append(lax.slice_in_dim(out, at, at + a.shape[along], axis=along))
        at += a.shape[along]
    return tuple(outs)


def document_of(positions, starts):
    return jnp.sum((positions[:, None] >= starts[None, :]).astype(jnp.int32), axis=1)


def absorb_block(state, q_half, allowed, k_block, v_block, kv_heads):
    running_max, running_sum, accum = state
    count = k_block.shape[0]
    k_heads = k_block.reshape(count, kv_heads, HEAD_SIZE)
    v_heads = v_block.reshape(count, kv_heads, HEAD_SIZE)
    scores = jnp.einsum(
        "qgrd,kgd->grqk", q_half, k_heads, preferred_element_type=jnp.float32
    ) * HEAD_SIZE ** (-0.5)
    scores = jnp.where(allowed[None, None], scores, jnp.float32(-1e30))
    new_max = jnp.maximum(running_max, jnp.max(scores, axis=-1))
    correction = jnp.exp(running_max - new_max)
    expo = jnp.where(allowed[None, None], jnp.exp(scores - new_max[..., None]), jnp.float32(0.0))
    new_sum = running_sum * correction + jnp.sum(expo, axis=-1)
    product = jnp.einsum(
        "grqk,kgd->grqd", expo.astype(jnp.bfloat16), v_heads, preferred_element_type=jnp.float32
    )
    return (new_max, new_sum, accum * correction[..., None] + product)


def shards(queries, keys, values, doc_lengths):
    local_q, local_k, local_v = (
        lax.all_to_all(queries, "kvh", split_axis=1, concat_axis=0, tiled=True),
        lax.all_to_all(keys, "kvh", split_axis=1, concat_axis=0, tiled=True),
        lax.all_to_all(values, "kvh", split_axis=1, concat_axis=0, tiled=True),
    )
    tok = local_q.shape[0]
    half = tok // 2
    place = lax.axis_index(CTX)
    kv_heads = local_k.shape[1] // HEAD_SIZE
    query_group = local_q.shape[1] // local_k.shape[1]
    starts = jnp.cumsum(doc_lengths) - doc_lengths
    offsets = jnp.arange(half, dtype=jnp.int32)
    lower_pos = place * tok + offsets
    upper_q = local_q[half:]
    upper_pos = place * tok + half + offsets
    segments = []
    for rows, positions in ((local_q[:half], lower_pos), (upper_q, upper_pos)):
        segments.append(
            (
                rows.reshape(half, kv_heads, query_group, HEAD_SIZE),
                positions,
                document_of(positions, starts),
            )
        )

    def absorb_all(states, k_block, v_block, k_pos):
        k_doc = document_of(k_pos, starts)
        updated = []
        for (q_half, q_pos, q_doc), state in zip(segments, states):
            causal = k_pos[None, :] <= q_pos[:, None]
            same_doc = q_doc[:, None] == k_doc[None, :]
            allowed = causal & (same_doc | (k_pos[None, :] < SINK))
            state = lax.cond(
                jnp.any(allowed),
                lambda s: absorb_block(s, q_half, allowed, k_block, v_block, kv_heads),
                lambda s: s,
                state,
            )
            updated.append(state)
        return tuple(updated)

    empty = (
        jnp.full((kv_heads, query_group, half), -1e30, jnp.float32),
        jnp.zeros((kv_heads, query_group, half), jnp.float32),
        jnp.zeros((kv_heads, query_group, half, HEAD_SIZE), jnp.float32),
    )
    states = (empty, empty)
    carry = states
    k_piece, v_piece = side_by_side((local_k, local_v), CTX, 0, 1)
    count = k_piece.shape[0]
    block = 512

    def inner(state, number):
        first = number * block
        k_block = lax.dynamic_slice_in_dim(k_piece, first, block, 0)
        v_block = lax.dynamic_slice_in_dim(v_piece, first, block, 0)
        k_pos = first + jnp.arange(block, dtype=jnp.int32)
        return (absorb_all(state, k_block, v_block, k_pos), None)

    carry, unused = lax.scan(inner, carry, jnp.arange(count // block, dtype=jnp.int32))
    states = carry
    outputs = []
    for running_max, running_sum, accum in states:
        normed = accum / running_sum[..., None]
        outputs.append(
            jnp.transpose(normed, (2, 0, 1, 3))
            .reshape(half, kv_heads * query_group * HEAD_SIZE)
            .astype(jnp.bfloat16)
        )
    lower_out, upper_out = outputs
    merged = jnp.concatenate([lower_out, upper_out], axis=0)
    return lax.all_to_all(merged, "kvh", split_axis=0, concat_axis=1, tiled=True)


def solution(mesh):
    torus = Mesh(
        mesh.devices.reshape(2, 4, 8, mesh.shape["kvh"]), ("ctx_0", "ctx_1", "ctx_2", "kvh")
    )
    in_specs = (P(CTX_KVH, None), P(CTX_KVH, None), P(CTX_KVH, None), P())
    out_specs = P(CTX_KVH, None)
    return jax.shard_map(
        shards, mesh=torus, in_specs=in_specs, out_specs=out_specs, check_vma=False
    )
```

profile of v0, /device:TPU:114, one launch (start us, length us, event | category | flops | bytes accessed | tf_op | source)
XLA Modules:
  0.0 528.9 jit_solution(15424428475770171093)
XLA Ops:
  8.0 3.4 all-to-all-start
  12.3 4.8 all-to-all-done
  17.0 8.0 %all_to_all.73 = bf16[64,4,128]{2,0,1:T(8,128)(2,1)S(1)} all-to-all(bf16[64,4,128]{2,0,1:T(8,128)(2,1)S(1)} %copy_bitcast_fusion.1), channel_id=1, replica_groups=mesh['ctx_0'=2,'ctx_1'=4,'ctx_2'=8,'kvh'=4] {'kvh'}, dimensions={1} | all-to-all | bytes 131072 | tf_op jit(solution)/shard_map/all_to_all | solution.py:49
  25.7 1.7 copy.54
  27.4 3.4 all-to-all-start.2
  32.5 5.9 %all-to-all-done.2 = bf16[64,4,512]{2,0,1:T(8,128)(2,1)S(1)} async-done(((bf16[64,4,512]{2,0,1:T(8,128)(2,1)}), bf16[64,4,512]{2,0,1:T(8,128)(2,1)S(1)}, u32[]{:S(2)}, u32[]{:S(2)}) %all-to-all-start.2) | async-done | bytes 262176 | tf_op jit(solution)/shard_map/all_to_all | solution.py:47
  38.5 282.3 %all-gather.2.cloned.1.call-done = bf16[16384,256]{1,0:T(8,128)(2,1)} async-done(((bf16[256,256]{1,0:T(8,128)(2,1)}), bf16[16384,256]{1,0:T(8,128)(2,1)}) %all-gather.2.cloned.1.call-update) | async-done | bytes 8388624 | tf_op jit(solution)/shard_map/all_gather | solution.py:15
  320.8 5.7 %fusion.38 = (bf16[16384,128]{1,0:T(8,128)(2,1)}, bf16[16384,128]{1,0:T(8,128)(2,1)}) fusion(bf16[16384,256]{1,0:T(8,128)(2,1)} %all-gather.2.cloned.1.call-done), kind=kLoop, calls=%fused_computation.66 | loop fusion | bytes 16777216 | tf_op jit(solution)/shard_map/slice | solution.py:17
  326.6 183.6 %while.21 = (s32[]{:T(128)}, f32[1,4,128]{2,1,0:T(4,128)S(1)}, f32[1,4,128]{2,1,0:T(4,128)S(1)}, f32[1,4,128,128]{3,2,1,0:T(8,128)S(1)}, f32[1,4,128]{2,1,0:T(4,...) while((s32[]{:T(128)}, f32[1,4,128]{2,1,0:T(4,128)S(1)}, ...), condition=%wide.region_15.16_spmd.clone, body=%wide.region_3.15_spmd.clone.sunk | while | flops 274100480 | bytes 9255479 | solution.py:105
  330.6 1.0 conditional.7
  385.8 1.0 conditional.7
  387.4 1.0 conditional.6
  392.5 1.0 conditional.7
  399.2 1.0 conditional.7
  405.9 1.0 conditional.7
  412.6 1.0 conditional.7
  419.3 1.0 conditional.7
  432.7 1.0 conditional.7
  439.4 1.0 conditional.7
  452.9 1.0 conditional.7
  459.6 1.0 conditional.7
  473.0 1.0 conditional.7
  479.7 1.0 conditional.7
  510.7 10.6 %all_to_all.74 = bf16[4,64,512]{2,1,0:T(8,128)(2,1)S(1)} all-to-all(bf16[4,64,512]{2,1,0:T(8,128)(2,1)S(1)} %bitcast.110), channel_id=1, replica_groups=mesh['ctx_0'=2,'ctx_1'=4,'ctx_2'=8,'kvh'=4] {'kvh'}, dimensions={0} | all-to-all | bytes 524288 | tf_op jit(solution)/shard_map/all_to_all | solution.py:117
  (510 shorter events, 146.5 us)
Async XLA Ops:
  6.5 0.8 copy-start
  8.0 9.0 %all-to-all-start = ((bf16[64,4,128]{2,0,1:T(8,128)(2,1)}), bf16[64,4,128]{2,0,1:T(8,128)(2,1)S(1)}, u32[]{:S(2)}, u32[]{:S(2)}) async-start(bf16[64,4,128]{2,0,1:T(8,128)(2,1)} %copy_bitcast_fusion.2), calls=%async_computation | async-start | bytes 131072 | tf_op jit(solution)/shard_map/all_to_all | solution.py:48
  11.4 309.4 %all-gather.2.cloned.1.call-start = ((), (), s32[]{:S(2)}) async-start(), calls=%async_computation.4 | async-start | bytes 8519680 | tf_op jit(solution)/shard_map/all_gather | solution.py:15
  27.4 10.9 %all-to-all-start.2 = ((bf16[64,4,512]{2,0,1:T(8,128)(2,1)}), bf16[64,4,512]{2,0,1:T(8,128)(2,1)S(1)}, u32[]{:S(2)}, u32[]{:S(2)}) async-start(bf16[64,4,512]{2,0,1:T(8,128)(2,1)} %bitcast.102), calls=%async_computation.2 | async-start | bytes 524288 | tf_op jit(solution)/shard_map/all_to_all | solution.py:47
Sparse Core Ops, SparseCore 0:
  25.8 294.8 all-gather.1
where the time goes:
time: 531 us; the launch traced here: 529 us
  waiting for transfers between devices  293 us (55%)
  loops' own time  64.4 us (12%)
  local copies, waits for them, and re-layouts  62.1 us (12%)
  other arithmetic  44.3 us (8%)
  matrix products  26.2 us (5%)
  blocking collectives  18.6 us (4%)
  between operations  13.5 us (3%)
  starting transfers between devices  6.8 us (1%)
    all_gather x1, waiting for transfers between devices, side_by_side(): out, at, outs = (lax.all_gather(both, axis, axis=dim, tiled=True), 0, [])  282 us
    another operation x1, loops' own time, shards(): lax.scan(inner, carry, jnp.arange(count // block, dtype=jnp.int32))  62.6 us
    reduce_or x32, other arithmetic, absorb_all(): jnp.any(allowed)  31.5 us
    dynamic_slice x32, local copies, waits for them, and re-layouts, inner(): v_block = lax.dynamic_slice_in_dim(v_piece, first, block, 0)  31.5 us
    dynamic_slice x32, local copies, waits for them, and re-layouts, shards(): lax.scan(inner, carry, jnp.arange(count // block, dtype=jnp.int32))  18.8 us
    dot_general x34, matrix products, absorb_block(): jnp.einsum('grqk,kgd->grqd', expo.astype(jnp.bfloat16), v_heads, preferre...  15.6 us
    all_to_all x1, blocking collectives, shards(): lax.all_to_all(merged, 'kvh', split_axis=0, concat_axis=1, tiled=True)  10.6 us
  transfers between devices with their start and end apart: 3, of which 3 were waited for; matrix products, arithmetic and copies ran while one was open for 1% of the time, Pallas kernels for 0%

commit v1 on v0

v1 whole, which is shorter than its diff:
```python
import functools

import jax
import jax.numpy as jnp
from jax import lax
from jax.experimental import pallas as pl
from jax.experimental.pallas import tpu as pltpu
from jax.sharding import Mesh
from jax.sharding import PartitionSpec as P

HEAD = 128
SINK = 128
GROUP = ("ctx_0", "ctx_1")
RING = "ctx_2"
CTX_KVH = ("ctx_0", "ctx_1", "ctx_2", "kvh")
N_GROUPS, N_RING = 8, 8
REACH = 4
BLOCK = 256
GROUP_KEYS = N_RING * BLOCK
NEG = -1e30
LOG2E = 1.4426950408889634
SCALE = HEAD**-0.5 * LOG2E


def fill_start_of(meta_ref, q_pos):
    start = jnp.zeros(q_pos.shape, jnp.int32)
    at = jnp.int32(0)
    for i in range(15):
        at = at + meta_ref[2 + i]
        start = jnp.where(q_pos >= at, at, start)
    return start


def first_start(meta_ref, pos):
    start, at = jnp.int32(0), jnp.int32(0)
    for i in range(15):
        at = at + meta_ref[2 + i]
        start = jnp.where(pos >= at, at, start)
    return start


def attend(d, meta_ref, q_ref, *refs):
    own = d == 0
    n_in = 9 + own
    blocks, (out_ref, k_ref, v_ref, s_ref) = refs[:n_in], refs[n_in:]
    heads = q_ref.shape[1] // HEAD
    n_keys = k_ref.shape[0]
    g, z = meta_ref[0], meta_ref[1]
    q_first = (g + d) * GROUP_KEYS + z * BLOCK
    key_first = g * GROUP_KEYS
    reach = first_start(meta_ref, q_first)
    active = (g + d < N_GROUPS) & ((g == 0) | (reach < key_first + GROUP_KEYS)) if d else True

    def run():
        places = (0, 1, 7, 2, 6, 3, 5)
        v_ref[:, HEAD:] = jnp.ones((n_keys, HEAD), v_ref.dtype)
        for ref, r in zip(blocks[:7], places):
            k_ref[r * BLOCK : (r + 1) * BLOCK, :] = ref[:, :HEAD]
            v_ref[r * BLOCK : (r + 1) * BLOCK, :HEAD] = ref[:, HEAD:]
        for i, ref in enumerate(blocks[7:9]):
            at = 4 * BLOCK + i * (BLOCK // 2)
            k_ref[at : at + BLOCK // 2, :] = ref[:, :HEAD]
            v_ref[at : at + BLOCK // 2, :HEAD] = ref[:, HEAD:]
        if own:
            k_ref[GROUP_KEYS:, :] = blocks[9][:, :HEAD]
            v_ref[GROUP_KEYS:, :HEAD] = blocks[9][:, HEAD:]
        q_pos = q_first + lax.broadcasted_iota(jnp.int32, (BLOCK, 1), 0)
        start = fill_start_of(meta_ref, q_pos)
        lane = lax.broadcasted_iota(jnp.int32, (1, BLOCK), 1)
        lane_out = lax.broadcasted_iota(jnp.int32, (BLOCK, HEAD), 1)
        stats = jnp.zeros((BLOCK, HEAD), jnp.float32)
        for h in range(heads):
            cols = slice(h * HEAD, (h + 1) * HEAD)
            top = jnp.full((BLOCK, HEAD), NEG, jnp.float32)
            q = q_ref[:, cols]
            for r in range(n_keys // BLOCK + (1 if n_keys % BLOCK else 0)):
                rows = slice(r * BLOCK, min((r + 1) * BLOCK, n_keys))
                width = rows.stop - rows.start
                s = lax.dot_general(
                    q, k_ref[rows, :], (((1,), (1,)), ((), ())), preferred_element_type=jnp.float32
                )
                if r < N_RING:
                    k_pos = key_first + lax.rem(z - r + N_RING, N_RING) * BLOCK + lane
                    seen = (k_pos >= start) | (k_pos < SINK)
                    if own:
                        seen = seen & (k_pos <= q_pos)
                    s = jnp.where(seen, s, NEG)
                else:
                    s = jnp.where(g > REACH, s, NEG)
                s_ref[:, rows] = s
                for c in range(0, width, HEAD):
                    top = jnp.maximum(top, s[:, c : c + HEAD])
            m = jnp.max(top, axis=1, keepdims=True) * SCALE
            p = jnp.exp2(s_ref[...] * SCALE - m).astype(jnp.bfloat16)
            o = jnp.dot(p, v_ref[...], preferred_element_type=jnp.float32)
            total = o[:, HEAD : HEAD + 1]
            out_ref[:, cols] = (o[:, :HEAD] / o[:, HEAD:]).astype(out_ref.dtype)
            lse = m + jnp.log2(total)
            for i in range(1 if own else 3):
                word = lse if own else lse.astype(jnp.bfloat16).astype(jnp.float32)
                stats = jnp.where(lane_out == 3 * h + i, word, stats)
                lse = lse - word
        out_ref[:, heads * HEAD :] = stats.astype(out_ref.dtype)

    if own:
        run()
    else:
        pl.when(active)(run)

        @pl.when(jnp.logical_not(active))
        def _():
            out_ref[:, : heads * HEAD] = jnp.zeros((BLOCK, heads * HEAD), out_ref.dtype)
            lane_out = lax.broadcasted_iota(jnp.int32, (BLOCK, HEAD), 1)
            out_ref[:, heads * HEAD :] = jnp.where(lane_out % 3 == 0, NEG, 0.0).astype(out_ref.dtype)


def merge(meta_ref, own_ref, *refs):
    parts, out_ref = refs[:REACH], refs[REACH]
    g = meta_ref[0]
    heads = out_ref.shape[1] // HEAD
    base = heads * HEAD
    for h in range(heads):
        cols = slice(h * HEAD, (h + 1) * HEAD)
        lses = [own_ref[:, base + 3 * h : base + 3 * h + 1]]
        for d, ref in enumerate(parts, 1):
            words = ref[:, base:].astype(jnp.float32)
            lse = words[:, 3 * h : 3 * h + 1] + words[:, 3 * h + 1 : 3 * h + 2] + words[:, 3 * h + 2 : 3 * h + 3]
            lses.append(jnp.where(g >= d, lse, NEG))
        top = functools.reduce(jnp.maximum, lses)
        weights = [jnp.exp2(x - top) for x in lses]
        total = functools.reduce(jnp.add, weights)
        acc = own_ref[:, cols] * (weights[0] / total)
        for w, ref in zip(weights[1:], parts):
            acc = acc + ref[:, cols].astype(jnp.float32) * (w / total)
        out_ref[:, cols] = acc.astype(out_ref.dtype)


VMEM = pl.BlockSpec(memory_space=pltpu.VMEM)
SMEM = pl.BlockSpec(memory_space=pltpu.SMEM)


def attend_call(d, meta, q, blocks):
    n_keys = GROUP_KEYS + (SINK if d == 0 else 0)
    width = q.shape[1]
    return pl.pallas_call(
        functools.partial(attend, d),
        name=f"attend_{d}",
        out_shape=jax.ShapeDtypeStruct((BLOCK, width + HEAD), jnp.float32 if d == 0 else jnp.bfloat16),
        in_specs=[SMEM] + [VMEM] * (1 + len(blocks)),
        out_specs=VMEM,
        scratch_shapes=[
            pltpu.VMEM((n_keys, HEAD), jnp.bfloat16),
            pltpu.VMEM((n_keys, 2 * HEAD), jnp.bfloat16),
            pltpu.VMEM((BLOCK, n_keys), jnp.float32),
        ],
        compiler_params=pltpu.CompilerParams(vmem_limit_bytes=24 << 20),
        cost_estimate=pl.CostEstimate(
            flops=6 * BLOCK * n_keys * width,
            transcendentals=BLOCK * n_keys * width // HEAD,
            bytes_accessed=4 << 20,
        ),
    )(meta, q, *blocks)


def merge_call(meta, own, parts):
    width = own.shape[1] - HEAD
    return pl.pallas_call(
        merge,
        name="merge",
        out_shape=jax.ShapeDtypeStruct((BLOCK, width), jnp.bfloat16),
        in_specs=[SMEM] + [VMEM] * (1 + len(parts)),
        out_specs=VMEM,
        compiler_params=pltpu.CompilerParams(vmem_limit_bytes=16 << 20),
    )(meta, own, *parts)


def along_ring(x, step):
    return lax.ppermute(x, RING, [(i, (i + step) % N_RING) for i in range(N_RING)])


def to_group(x, step):
    return lax.ppermute(x, GROUP, [(i, i + step) for i in range(N_GROUPS) if 0 <= i + step < N_GROUPS])


def shards(queries, keys, values, doc_lengths):
    rows = queries.shape[0]
    kv_heads = keys.shape[1] // HEAD
    by_head = jnp.concatenate([x.reshape(rows, kv_heads, -1) for x in (queries, keys, values)], axis=2)
    mine = lax.all_to_all(by_head.reshape(rows, -1), "kvh", split_axis=1, concat_axis=0, tiled=True)
    width = queries.shape[1] // kv_heads
    q, kv = mine[:, :width], mine[:, width:]
    g, z = lax.axis_index(GROUP), lax.axis_index(RING)
    meta = jnp.concatenate([jnp.stack([g, z]).astype(jnp.int32), doc_lengths])

    half = BLOCK // 2
    visiting = {}
    blocks, up, down = [kv], kv, kv
    for step in range(3):
        up, down = along_ring(up, 1), along_ring(down, -1)
        visiting[REACH - step] = to_group(q, step - REACH)
        blocks += [up, down]
    blocks += [along_ring(up[:half], 1), along_ring(down[half:], -1)]
    visiting[1] = to_group(q, -1)

    held = jnp.stack([b[:half] for b in blocks[:7]] + [blocks[7]])
    place = jnp.array([0, 1, 3, 5, 7, 6, 4, 2])[z]
    first = lax.dynamic_index_in_dim(held, place, 0, keepdims=False)
    sink = first * 0
    for far in range(REACH + 1, N_GROUPS):
        got = lax.ppermute(first, GROUP, [(0, far)])
        sink = jnp.where(g == far, got, sink)

    parts = []
    for d in range(REACH, 0, -1):
        parts.insert(0, to_group(attend_call(d, meta, visiting[d], blocks), d))
    own = attend_call(0, meta, q, blocks + [sink])
    out = merge_call(meta, own, parts)
    return lax.all_to_all(out, "kvh", split_axis=0, concat_axis=1, tiled=True)


def solution(mesh):
    torus = Mesh(mesh.devices.reshape(2, 4, 8, mesh.shape["kvh"]), CTX_KVH)
    in_specs = (P(CTX_KVH, None), P(CTX_KVH, None), P(CTX_KVH, None), P())
    return jax.shard_map(
        shards, mesh=torus, in_specs=in_specs, out_specs=P(CTX_KVH, None), check_vma=False
    )
```

time: 531 us -> 115 us (0.22)
  the two profiles are of different devices: /device:TPU:114 before, /device:TPU:1 now
where the time goes in v1:
time: 115 us; the launch traced here: 113 us
  starting transfers between devices  36.5 us (32%)
  waiting for transfers between devices  26.1 us (23%)
  Pallas kernels  26.1 us (23%)
  blocking collectives  17.7 us (15%)
  local copies, waits for them, and re-layouts  3.8 us (3%)
  between operations  2.25 us (2%)
    pallas_call x5, Pallas kernels, attend_call(): pl.pallas_call(functools.partial(attend, d), name=f'attend_{d}', out_shap...  23.5 us
    ppermute x8, waiting for transfers between devices, along_ring(): lax.ppermute(x, RING, [(i, (i + step) % N_RING) for i in range(N_RING)])  21.9 us
    all_to_all x1, blocking collectives, shards(): return lax.all_to_all(out, 'kvh', split_axis=0, concat_axis=1, tiled=True)  17.7 us
    ppermute x3, starting transfers between devices, shards(): got = lax.ppermute(first, GROUP, [(0, far)])  13.1 us
    ppermute x8, starting transfers between devices, to_group(): lax.ppermute(x, GROUP, [(i, i + step) for i in range(N_GROUPS) if 0 <= i...  10.4 us
    all_to_all x1, starting transfers between devices, shards(): lax.all_to_all(by_head.reshape(rows, -1), 'kvh', split_axis=1, concat_axi...  6.67 us
    ppermute x8, starting transfers between devices, along_ring(): lax.ppermute(x, RING, [(i, (i + step) % N_RING) for i in range(N_RING)])  6.33 us
    all_to_all x1, waiting for transfers between devices, shards(): lax.all_to_all(by_head.reshape(rows, -1), 'kvh', split_axis=1, concat_axi...  4.16 us
  transfers between devices with their start and end apart: 20, of which 6 were waited for; matrix products, arithmetic and copies ran while one was open for 1% of the time, Pallas kernels for 21%

profile of v1, /device:TPU:1, one launch (start us, length us, event | category | flops | bytes accessed | tf_op | source)
XLA Modules:
  0.0 113.3 jit_solution(14933256017127084596)
XLA Ops:
  1.8 6.7 %all-to-all-start = ((bf16[64,4,768]{2,0,1:T(8,128)(2,1)}), bf16[64,4,768]{2,0,1:T(8,128)(2,1)S(1)}, u32[]{:S(2)}, u32[]{:S(2)}) async-start(bf16[64,4,768]{2,0,1:T(8,128)(2,1)} %pad_maximum_fusion), calls=%async_computation | async-start | bytes 786432 | tf_op jit(solution)/shard_map/all_to_all | solution.py:189
  12.4 4.2 %all-to-all-done = bf16[64,4,768]{2,0,1:T(8,128)(2,1)S(1)} async-done(((bf16[64,4,768]{2,0,1:T(8,128)(2,1)}), bf16[64,4,768]{2,0,1:T(8,128)(2,1)S(1)}, u32[]{:S(2)}, u32[]{:S(2)}) %all-to-all-start) | async-done | bytes 393248 | tf_op jit(solution)/shard_map/all_to_all | solution.py:189
  17.5 4.0 %collective-permute-start.1 = (bf16[256,256]{1,0:T(8,128)(2,1)S(1)}, bf16[256,256]{1,0:T(8,128)(2,1)S(1)}, u32[]{:S(2)}, u32[]{:S(2)}) collective-permute-start(bf16[256,256]{1,0:T(8,128)(2,1)S(1)} %slice.43.refs_0_), channel_id=1, source_target_pairs={{0,28},{4,0},{8,4},{12,8},{16,12},{20,16},{24,20},{28,24},{1,29},{... | collective-permute-start | bytes 393224 | tf_op jit(solution)/shard_map/ppermute | solution.py:178
  22.8 1.3 %collective-permute-start.13 = (bf16[256,512]{1,0:T(8,128)(2,1)S(1)}, bf16[256,512]{1,0:T(8,128)(2,1)S(1)}, u32[]{:S(2)}, u32[]{:S(2)}) collective-permute-start(bf16[256,512]{1,0:T(8,128)(2,1)S(1)} %slice.42.q_ref), channel_id=1, source_target_pairs={{64,0},{96,32},{128,64},{160,96},{192,128},{224,160},{65,1},{97,33... | collective-permute-start | bytes 786440 | tf_op jit(solution)/shard_map/ppermute | solution.py:182
  24.1 1.3 %collective-permute-start.15 = (bf16[256,512]{1,0:T(8,128)(2,1)S(1)}, bf16[256,512]{1,0:T(8,128)(2,1)S(1)}, u32[]{:S(2)}, u32[]{:S(2)}) collective-permute-start(bf16[256,512]{1,0:T(8,128)(2,1)S(1)} %slice.42.q_ref), channel_id=1, source_target_pairs={{96,0},{128,32},{160,64},{192,96},{224,128},{97,1},{129,33},{161,6... | collective-permute-start | bytes 786440 | tf_op jit(solution)/shard_map/ppermute | solution.py:182
  26.8 5.3 %collective-permute-done.2.refs_3_ = bf16[256,256]{1,0:T(8,128)(2,1)S(1)} collective-permute-done((bf16[256,256]{1,0:T(8,128)(2,1)S(1)}, bf16[256,256]{1,0:T(8,128)(2,1)S(1)}, u32[]{:S(2)}, u32[]{:S(2)}) %collective-permute-start.2) | collective-permute-done | bytes 131104 | tf_op jit(solution)/shard_map/ppermute | solution.py:178
  32.3 3.9 %collective-permute-done.3.refs_4_ = bf16[256,256]{1,0:T(8,128)(2,1)S(1)} collective-permute-done((bf16[256,256]{1,0:T(8,128)(2,1)S(1)}, bf16[256,256]{1,0:T(8,128)(2,1)S(1)}, u32[]{:S(2)}, u32[]{:S(2)}) %collective-permute-start.3) | collective-permute-done | bytes 131104 | tf_op jit(solution)/shard_map/ppermute | solution.py:178
  36.3 5.0 %collective-permute-done.4.refs_5_ = bf16[256,256]{1,0:T(8,128)(2,1)S(1)} collective-permute-done((bf16[256,256]{1,0:T(8,128)(2,1)S(1)}, bf16[256,256]{1,0:T(8,128)(2,1)S(1)}, u32[]{:S(2)}, u32[]{:S(2)}) %collective-permute-start.4) | collective-permute-done | bytes 131104 | tf_op jit(solution)/shard_map/ppermute | solution.py:178
  41.8 3.3 %collective-permute-done.5.refs_6_ = bf16[256,256]{1,0:T(8,128)(2,1)S(1)} collective-permute-done((bf16[256,256]{1,0:T(8,128)(2,1)S(1)}, bf16[256,256]{1,0:T(8,128)(2,1)S(1)}, u32[]{:S(2)}, u32[]{:S(2)}) %collective-permute-start.5) | collective-permute-done | bytes 131104 | tf_op jit(solution)/shard_map/ppermute | solution.py:178
  45.1 4.3 %collective-permute-done.6.refs_7_ = bf16[128,256]{1,0:T(8,128)(2,1)S(1)} collective-permute-done((bf16[128,256]{1,0:T(8,128)(2,1)S(1)}, bf16[128,256]{1,0:T(8,128)(2,1)S(1)}, u32[]{:S(2)}, u32[]{:S(2)}) %collective-permute-start.6) | collective-permute-done | bytes 65568 | tf_op jit(solution)/shard_map/ppermute | solution.py:178
  50.2 9.6 %collective-permute-start.8 = (bf16[128,256]{1,0:T(8,128)(2,1)S(1)}, bf16[128,256]{1,0:T(8,128)(2,1)S(1)}, u32[]{:S(2)}, u32[]{:S(2)}) collective-permute-start(bf16[128,256]{1,0:T(8,128)(2,1)S(1)} %dynamic-slice_bitcast_fusion), channel_id=1, source_target_pairs={{0,224},{1,225},{2,226},{3,227},{4,228},{5,229},{6,230},{7,231},{8... | collective-permute-start | bytes 196616 | tf_op jit(solution)/shard_map/ppermute | solution.py:210
  59.8 2.2 %collective-permute-start.9 = (bf16[128,256]{1,0:T(8,128)(2,1)S(1)}, bf16[128,256]{1,0:T(8,128)(2,1)S(1)}, u32[]{:S(2)}, u32[]{:S(2)}) collective-permute-start(bf16[128,256]{1,0:T(8,128)(2,1)S(1)} %dynamic-slice_bitcast_fusion), channel_id=1, source_target_pairs={{0,192},{1,193},{2,194},{3,195},{4,196},{5,197},{6,198},{7,199},{8... | collective-permute-start | bytes 196616 | tf_op jit(solution)/shard_map/ppermute | solution.py:210
  62.0 4.7 %attend_1.1 = bf16[256,640]{1,0:T(8,128)(2,1)S(1)} custom-call(s32[18]{0:T(128)S(1)} %pad_add_fusion.meta_ref, bf16[256,512]{1,0:T(8,128)(2,1)S(1)} %collective-permute-done.11.q_ref, bf16[256,256]{1,0:T(8,128)(2,1)S(1)} %slice.43.refs_0_, bf16[256,256]{1,0:T(8,128)(2,1)S(1)} %collective-permute-done.refs_1_, ...), custom_call_target="tpu_custom_call" | custom-call | flops 1610612736 | bytes 4194304 | tf_op jit(solution)/shard_map/attend_1/pallas_call | solution.py:145
  66.7 1.3 %collective-permute-start.10 = (bf16[128,256]{1,0:T(8,128)(2,1)S(1)}, bf16[128,256]{1,0:T(8,128)(2,1)S(1)}, u32[]{:S(2)}, u32[]{:S(2)}) collective-permute-start(bf16[128,256]{1,0:T(8,128)(2,1)S(1)} %dynamic-slice_bitcast_fusion), channel_id=1, source_target_pairs={{0,160},{1,161},{2,162},{3,163},{4,164},{5,165},{6,166},{7,167},{8... | collective-permute-start | bytes 196616 | tf_op jit(solution)/shard_map/ppermute | solution.py:210
  68.0 4.8 %attend_2.1 = bf16[256,640]{1,0:T(8,128)(2,1)S(1)} custom-call(s32[18]{0:T(128)S(1)} %pad_add_fusion.meta_ref, bf16[256,512]{1,0:T(8,128)(2,1)S(1)} %collective-permute-done.13.q_ref, bf16[256,256]{1,0:T(8,128)(2,1)S(1)} %slice.43.refs_0_, bf16[256,256]{1,0:T(8,128)(2,1)S(1)} %collective-permute-done.refs_1_, ...), custom_call_target="tpu_custom_call" | custom-call | flops 1610612736 | bytes 4194304 | tf_op jit(solution)/shard_map/attend_2/pallas_call | solution.py:145
  72.9 1.3 %collective-permute-start.12 = (bf16[256,640]{1,0:T(8,128)(2,1)S(1)}, bf16[256,640]{1,0:T(8,128)(2,1)S(1)}, u32[]{:S(2)}, u32[]{:S(2)}) collective-permute-start(bf16[256,640]{1,0:T(8,128)(2,1)S(1)} %attend_1.1), channel_id=1, source_target_pairs={{0,32},{32,64},{64,96},{96,128},{128,160},{160,192},{192,224},{1,3... | collective-permute-start | bytes 983048 | tf_op jit(solution)/shard_map/ppermute | solution.py:182
  74.2 4.7 %attend_3.1 = bf16[256,640]{1,0:T(8,128)(2,1)S(1)} custom-call(s32[18]{0:T(128)S(1)} %pad_add_fusion.meta_ref, bf16[256,512]{1,0:T(8,128)(2,1)S(1)} %collective-permute-done.15.q_ref, bf16[256,256]{1,0:T(8,128)(2,1)S(1)} %slice.43.refs_0_, bf16[256,256]{1,0:T(8,128)(2,1)S(1)} %collective-permute-done.refs_1_, ...), custom_call_target="tpu_custom_call" | custom-call | flops 1610612736 | bytes 4194304 | tf_op jit(solution)/shard_map/attend_3/pallas_call | solution.py:145
  78.9 1.3 %collective-permute-start.14 = (bf16[256,640]{1,0:T(8,128)(2,1)S(1)}, bf16[256,640]{1,0:T(8,128)(2,1)S(1)}, u32[]{:S(2)}, u32[]{:S(2)}) collective-permute-start(bf16[256,640]{1,0:T(8,128)(2,1)S(1)} %attend_2.1), channel_id=1, source_target_pairs={{0,64},{32,96},{64,128},{96,160},{128,192},{160,224},{1,65},{33,97... | collective-permute-start | bytes 983048 | tf_op jit(solution)/shard_map/ppermute | solution.py:182
  80.2 4.9 %attend_4.1 = bf16[256,640]{1,0:T(8,128)(2,1)S(1)} custom-call(s32[18]{0:T(128)S(1)} %pad_add_fusion.meta_ref, bf16[256,512]{1,0:T(8,128)(2,1)S(1)} %collective-permute-done.17.q_ref, bf16[256,256]{1,0:T(8,128)(2,1)S(1)} %slice.43.refs_0_, bf16[256,256]{1,0:T(8,128)(2,1)S(1)} %collective-permute-done.refs_1_, ...), custom_call_target="tpu_custom_call" | custom-call | flops 1610612736 | bytes 4194304 | tf_op jit(solution)/shard_map/attend_4/pallas_call | solution.py:145
  85.1 1.3 %collective-permute-start.16 = (bf16[256,640]{1,0:T(8,128)(2,1)S(1)}, bf16[256,640]{1,0:T(8,128)(2,1)S(1)}, u32[]{:S(2)}, u32[]{:S(2)}) collective-permute-start(bf16[256,640]{1,0:T(8,128)(2,1)S(1)} %attend_3.1), channel_id=1, source_target_pairs={{0,96},{32,128},{64,160},{96,192},{128,224},{1,97},{33,129},{65,16... | collective-permute-start | bytes 983048 | tf_op jit(solution)/shard_map/ppermute | solution.py:182
  86.4 1.3 %collective-permute-start.18 = (bf16[256,640]{1,0:T(8,128)(2,1)S(1)}, bf16[256,640]{1,0:T(8,128)(2,1)S(1)}, u32[]{:S(2)}, u32[]{:S(2)}) collective-permute-start(bf16[256,640]{1,0:T(8,128)(2,1)S(1)} %attend_4.1), channel_id=1, source_target_pairs={{0,128},{32,160},{64,192},{96,224},{1,129},{33,161},{65,193},{97,2... | collective-permute-start | bytes 983048 | tf_op jit(solution)/shard_map/ppermute | solution.py:182
  87.8 4.5 %attend_0.1.own_ref = f32[256,640]{1,0:T(8,128)S(1)} custom-call(s32[18]{0:T(128)S(1)} %pad_add_fusion.meta_ref, bf16[256,512]{1,0:T(8,128)(2,1)S(1)} %slice.42.q_ref, bf16[256,256]{1,0:T(8,128)(2,1)S(1)} %slice.43.refs_0_, bf16[256,256]{1,0:T(8,128)(2,1)S(1)} %collective-permute-done.refs_1_, bf16[256,256]{1,0:T(8,128)(2,1)S(1)} %collective-permute-done.1.refs_2_, ...), custom_call_target="tpu_custom_call" | custom-call | flops 1711276032 | bytes 4194304 | tf_op jit(solution)/shard_map/attend_0/pallas_call | solution.py:145
  92.3 2.6 %merge.1 = bf16[256,512]{1,0:T(8,128)(2,1)S(1)} custom-call(s32[18]{0:T(128)S(1)} %pad_add_fusion.meta_ref, f32[256,640]{1,0:T(8,128)S(1)} %attend_0.1.own_ref, bf16[256,640]{1,0:T(8,128)(2,1)S(1)} %collective-permute-done.12.refs_0_, bf16[256,640]{1,0:T(8,128)(2,1)S(1)} %collective-permute-done.14.refs_1_, ...), custom_call_target="tpu_custom_call" | custom-call | tf_op jit(solution)/shard_map/merge/pallas_call | solution.py:167
  94.9 17.7 %all_to_all.35 = bf16[4,64,512]{2,1,0:T(8,128)(2,1)S(1)} all-to-all(bf16[4,64,512]{2,1,0:T(8,128)(2,1)S(1)} %bitcast.56), channel_id=1, replica_groups=mesh['ctx_0'=2,'ctx_1'=4,'ctx_2'=8,'kvh'=4] {'kvh'}, dimensions={0} | all-to-all | bytes 524288 | tf_op jit(solution)/shard_map/all_to_all | solution.py:218
  (51 shorter events, 9.6 us)
Async XLA Ops:
  0.0 1.0 copy-start
  0.0 1.0 copy-start.1
  1.8 14.7 %all-to-all-start = ((bf16[64,4,768]{2,0,1:T(8,128)(2,1)}), bf16[64,4,768]{2,0,1:T(8,128)(2,1)S(1)}, u32[]{:S(2)}, u32[]{:S(2)}) async-start(bf16[64,4,768]{2,0,1:T(8,128)(2,1)} %pad_maximum_fusion), calls=%async_computation | async-start | bytes 786432 | tf_op jit(solution)/shard_map/all_to_all | solution.py:189
  8.5 0.7 copy-start.3
  11.7 0.7 copy-start.2
  16.6 8.8 %collective-permute-start = (bf16[256,256]{1,0:T(8,128)(2,1)S(1)}, bf16[256,256]{1,0:T(8,128)(2,1)S(1)}, u32[]{:S(2)}, u32[]{:S(2)}) collective-permute-start(bf16[256,256]{1,0:T(8,128)(2,1)S(1)} %slice.43.refs_0_), channel_id=1, source_target_pairs={{0,4},{4,8},{8,12},{12,16},{16,20},{20,24},{24,28},{28,0},{1,5},{5... | collective-permute-start | bytes 393224 | tf_op jit(solution)/shard_map/ppermute | solution.py:178
  17.5 9.3 %collective-permute-start.1 = (bf16[256,256]{1,0:T(8,128)(2,1)S(1)}, bf16[256,256]{1,0:T(8,128)(2,1)S(1)}, u32[]{:S(2)}, u32[]{:S(2)}) collective-permute-start(bf16[256,256]{1,0:T(8,128)(2,1)S(1)} %slice.43.refs_0_), channel_id=1, source_target_pairs={{0,28},{4,0},{8,4},{12,8},{16,12},{20,16},{24,20},{28,24},{1,29},{... | collective-permute-start | bytes 393224 | tf_op jit(solution)/shard_map/ppermute | solution.py:178
  21.5 28.7 %collective-permute-start.11 = (bf16[256,512]{1,0:T(8,128)(2,1)S(1)}, bf16[256,512]{1,0:T(8,128)(2,1)S(1)}, u32[]{:S(2)}, u32[]{:S(2)}) collective-permute-start(bf16[256,512]{1,0:T(8,128)(2,1)S(1)} %slice.42.q_ref), channel_id=1, source_target_pairs={{32,0},{64,32},{96,64},{128,96},{160,128},{192,160},{224,192},{33,... | collective-permute-start | bytes 786440 | tf_op jit(solution)/shard_map/ppermute | solution.py:182
  22.8 43.9 %collective-permute-start.13 = (bf16[256,512]{1,0:T(8,128)(2,1)S(1)}, bf16[256,512]{1,0:T(8,128)(2,1)S(1)}, u32[]{:S(2)}, u32[]{:S(2)}) collective-permute-start(bf16[256,512]{1,0:T(8,128)(2,1)S(1)} %slice.42.q_ref), channel_id=1, source_target_pairs={{64,0},{96,32},{128,64},{160,96},{192,128},{224,160},{65,1},{97,33... | collective-permute-start | bytes 786440 | tf_op jit(solution)/shard_map/ppermute | solution.py:182
  24.1 48.8 %collective-permute-start.15 = (bf16[256,512]{1,0:T(8,128)(2,1)S(1)}, bf16[256,512]{1,0:T(8,128)(2,1)S(1)}, u32[]{:S(2)}, u32[]{:S(2)}) collective-permute-start(bf16[256,512]{1,0:T(8,128)(2,1)S(1)} %slice.42.q_ref), channel_id=1, source_target_pairs={{96,0},{128,32},{160,64},{192,96},{224,128},{97,1},{129,33},{161,6... | collective-permute-start | bytes 786440 | tf_op jit(solution)/shard_map/ppermute | solution.py:182
  25.4 53.5 %collective-permute-start.17 = (bf16[256,512]{1,0:T(8,128)(2,1)S(1)}, bf16[256,512]{1,0:T(8,128)(2,1)S(1)}, u32[]{:S(2)}, u32[]{:S(2)}) collective-permute-start(bf16[256,512]{1,0:T(8,128)(2,1)S(1)} %slice.42.q_ref), channel_id=1, source_target_pairs={{128,0},{160,32},{192,64},{224,96},{129,1},{161,33},{193,65},{225,... | collective-permute-start | bytes 786440 | tf_op jit(solution)/shard_map/ppermute | solution.py:182
  26.7 5.4 %collective-permute-start.2 = (bf16[256,256]{1,0:T(8,128)(2,1)S(1)}, bf16[256,256]{1,0:T(8,128)(2,1)S(1)}, u32[]{:S(2)}, u32[]{:S(2)}) collective-permute-start(bf16[256,256]{1,0:T(8,128)(2,1)S(1)} %collective-permute-done.refs_1_), channel_id=1, source_target_pairs={{0,4},{4,8},{8,12},{12,16},{16,20},{20,24},{24,28},{28,0},{1,5},{5... | collective-permute-start | bytes 393224 | tf_op jit(solution)/shard_map/ppermute | solution.py:178
  32.1 4.1 %collective-permute-start.3 = (bf16[256,256]{1,0:T(8,128)(2,1)S(1)}, bf16[256,256]{1,0:T(8,128)(2,1)S(1)}, u32[]{:S(2)}, u32[]{:S(2)}) collective-permute-start(bf16[256,256]{1,0:T(8,128)(2,1)S(1)} %collective-permute-done.1.refs_2_), channel_id=1, source_target_pairs={{0,28},{4,0},{8,4},{12,8},{16,12},{20,16},{24,20},{28,24},{1,29},{... | collective-permute-start | bytes 393224 | tf_op jit(solution)/shard_map/ppermute | solution.py:178
  36.2 5.0 %collective-permute-start.4 = (bf16[256,256]{1,0:T(8,128)(2,1)S(1)}, bf16[256,256]{1,0:T(8,128)(2,1)S(1)}, u32[]{:S(2)}, u32[]{:S(2)}) collective-permute-start(bf16[256,256]{1,0:T(8,128)(2,1)S(1)} %collective-permute-done.2.refs_3_), channel_id=1, source_target_pairs={{0,4},{4,8},{8,12},{12,16},{16,20},{20,24},{24,28},{28,0},{1,5},{5... | collective-permute-start | bytes 393224 | tf_op jit(solution)/shard_map/ppermute | solution.py:178
  41.3 3.8 %collective-permute-start.5 = (bf16[256,256]{1,0:T(8,128)(2,1)S(1)}, bf16[256,256]{1,0:T(8,128)(2,1)S(1)}, u32[]{:S(2)}, u32[]{:S(2)}) collective-permute-start(bf16[256,256]{1,0:T(8,128)(2,1)S(1)} %collective-permute-done.3.refs_4_), channel_id=1, source_target_pairs={{0,28},{4,0},{8,4},{12,8},{16,12},{20,16},{24,20},{28,24},{1,29},{... | collective-permute-start | bytes 393224 | tf_op jit(solution)/shard_map/ppermute | solution.py:178
  45.1 4.3 %collective-permute-start.6 = (bf16[128,256]{1,0:T(8,128)(2,1)S(1)}, bf16[128,256]{1,0:T(8,128)(2,1)S(1)}, u32[]{:S(2)}, u32[]{:S(2)}) collective-permute-start(bf16[128,256]{1,0:T(8,128)(2,1)S(1)} %slice.44), channel_id=1, source_target_pairs={{0,4},{4,8},{8,12},{12,16},{16,20},{20,24},{24,28},{28,0},{1,5},{5... | collective-permute-start | bytes 196616 | tf_op jit(solution)/shard_map/ppermute | solution.py:178
  49.4 10.3 %collective-permute-start.7 = (bf16[128,256]{1,0:T(8,128)(2,1)S(1)}, bf16[128,256]{1,0:T(8,128)(2,1)S(1)}, u32[]{:S(2)}, u32[]{:S(2)}) collective-permute-start(bf16[128,256]{1,0:T(8,128)(2,1)S(1)} %slice.45), channel_id=1, source_target_pairs={{0,28},{4,0},{8,4},{12,8},{16,12},{20,16},{24,20},{28,24},{1,29},{... | collective-permute-start | bytes 196616 | tf_op jit(solution)/shard_map/ppermute | solution.py:178
  50.2 34.9 %collective-permute-start.8 = (bf16[128,256]{1,0:T(8,128)(2,1)S(1)}, bf16[128,256]{1,0:T(8,128)(2,1)S(1)}, u32[]{:S(2)}, u32[]{:S(2)}) collective-permute-start(bf16[128,256]{1,0:T(8,128)(2,1)S(1)} %dynamic-slice_bitcast_fusion), channel_id=1, source_target_pairs={{0,224},{1,225},{2,226},{3,227},{4,228},{5,229},{6,230},{7,231},{8... | collective-permute-start | bytes 196616 | tf_op jit(solution)/shard_map/ppermute | solution.py:210
  59.8 26.6 %collective-permute-start.9 = (bf16[128,256]{1,0:T(8,128)(2,1)S(1)}, bf16[128,256]{1,0:T(8,128)(2,1)S(1)}, u32[]{:S(2)}, u32[]{:S(2)}) collective-permute-start(bf16[128,256]{1,0:T(8,128)(2,1)S(1)} %dynamic-slice_bitcast_fusion), channel_id=1, source_target_pairs={{0,192},{1,193},{2,194},{3,195},{4,196},{5,197},{6,198},{7,199},{8... | collective-permute-start | bytes 196616 | tf_op jit(solution)/shard_map/ppermute | solution.py:210
  66.7 21.0 %collective-permute-start.10 = (bf16[128,256]{1,0:T(8,128)(2,1)S(1)}, bf16[128,256]{1,0:T(8,128)(2,1)S(1)}, u32[]{:S(2)}, u32[]{:S(2)}) collective-permute-start(bf16[128,256]{1,0:T(8,128)(2,1)S(1)} %dynamic-slice_bitcast_fusion), channel_id=1, source_target_pairs={{0,160},{1,161},{2,162},{3,163},{4,164},{5,165},{6,166},{7,167},{8... | collective-permute-start | bytes 196616 | tf_op jit(solution)/shard_map/ppermute | solution.py:210
  72.9 19.4 %collective-permute-start.12 = (bf16[256,640]{1,0:T(8,128)(2,1)S(1)}, bf16[256,640]{1,0:T(8,128)(2,1)S(1)}, u32[]{:S(2)}, u32[]{:S(2)}) collective-permute-start(bf16[256,640]{1,0:T(8,128)(2,1)S(1)} %attend_1.1), channel_id=1, source_target_pairs={{0,32},{32,64},{64,96},{96,128},{128,160},{160,192},{192,224},{1,3... | collective-permute-start | bytes 983048 | tf_op jit(solution)/shard_map/ppermute | solution.py:182
  78.9 13.4 %collective-permute-start.14 = (bf16[256,640]{1,0:T(8,128)(2,1)S(1)}, bf16[256,640]{1,0:T(8,128)(2,1)S(1)}, u32[]{:S(2)}, u32[]{:S(2)}) collective-permute-start(bf16[256,640]{1,0:T(8,128)(2,1)S(1)} %attend_2.1), channel_id=1, source_target_pairs={{0,64},{32,96},{64,128},{96,160},{128,192},{160,224},{1,65},{33,97... | collective-permute-start | bytes 983048 | tf_op jit(solution)/shard_map/ppermute | solution.py:182
  85.1 7.2 %collective-permute-start.16 = (bf16[256,640]{1,0:T(8,128)(2,1)S(1)}, bf16[256,640]{1,0:T(8,128)(2,1)S(1)}, u32[]{:S(2)}, u32[]{:S(2)}) collective-permute-start(bf16[256,640]{1,0:T(8,128)(2,1)S(1)} %attend_3.1), channel_id=1, source_target_pairs={{0,96},{32,128},{64,160},{96,192},{128,224},{1,97},{33,129},{65,16... | collective-permute-start | bytes 983048 | tf_op jit(solution)/shard_map/ppermute | solution.py:182
  86.4 5.9 %collective-permute-start.18 = (bf16[256,640]{1,0:T(8,128)(2,1)S(1)}, bf16[256,640]{1,0:T(8,128)(2,1)S(1)}, u32[]{:S(2)}, u32[]{:S(2)}) collective-permute-start(bf16[256,640]{1,0:T(8,128)(2,1)S(1)} %attend_4.1), channel_id=1, source_target_pairs={{0,128},{32,160},{64,192},{96,224},{1,129},{33,161},{65,193},{97,2... | collective-permute-start | bytes 983048 | tf_op jit(solution)/shard_map/ppermute | solution.py:182
